TPU v7x, 32 devices: a whole 2x2x4 slice. The times are simulated.
32 devices in a mesh: aux: 4 (over x, core), cd: 4 (over z), ab: 2 (over y).
Axes of the slice: x: 2, y: 2, z: 4, core: 2. Of those that a mesh axis runs over, the one named last changes fastest.
Arguments:
- left_integrals: bfloat16 [4, 2048, 2048], P('cd', 'ab', 'aux'), may hold values from -6 to 6
- right_integrals: bfloat16 [2, 2048, 2048], P('ab', 'cd', 'aux'), may hold values from -6 to 6
- metric_factor: bfloat16 [2048, 2048], P('aux'), may hold values from -0.125 to 0.125
- amplitudes: bfloat16 [32, 2048, 2048], P(None, 'ab', 'cd'), may hold values from -6.4373016e-05 to 6.4373016e-05
- tile_sizes: int32 [16], replicated, may hold values from 1 to 256, 2048 in all
- pair_mask: int32 [16, 16], replicated, may hold values 0 or 1
Outputs:
- ladder_residual: float32 [4, 2, 32], P('cd', 'ab')
Inputs may be any that keep to these rules, and one draw needn't show every extreme that they name: `tile_sizes`: the 16 tile sizes sum to 2048.
All inputs are finite; a program needn't handle non-finite values.
Results may differ from a plain program's by a relative error of at most 0.0038.
Values may be sent and summed in bfloat16 or wider, within the bound.
A program may use at most 128 MiB of HBM per device.

v0:
```python
import jax
import jax.numpy as jnp
from jax import lax
from jax.sharding import PartitionSpec as P


def region_keep(tile_sizes, pair_mask, c_offset, c_count, d_offset, d_count):
    tile_end = jnp.cumsum(tile_sizes)
    tile_range = jnp.arange(tile_end.shape[0], dtype=jnp.int32)

    def onehot(offset, count):
        positions = offset + jnp.arange(count, dtype=jnp.int32)
        tile_index = jnp.sum((positions[:, None] >= tile_end[None, :]).astype(jnp.int32), axis=1)
        return (tile_index[:, None] == tile_range[None, :]).astype(jnp.float32)

    left_hot = onehot(c_offset, c_count)
    right_hot = onehot(d_offset, d_count)
    mask_table = pair_mask.astype(jnp.float32)
    inner = jnp.dot(left_hot, mask_table, precision=lax.Precision.HIGHEST)
    return jnp.dot(inner, right_hot.T, precision=lax.Precision.HIGHEST)


def ladder_terms(left_piece, right_all, kept):
    aux_count = left_piece.shape[0]
    b_count = right_all.shape[1]
    d_width = right_all.shape[2]
    right_flat = right_all.reshape(aux_count, b_count * d_width)

    def one_virtual(left_slab):
        ladder = lax.dot_general(
            left_slab, right_flat, (((0,), (0,)), ((), ())), preferred_element_type=jnp.float32
        )
        ladder = ladder.astype(jnp.bfloat16).reshape(-1, b_count, d_width)
        total = lax.dot_general(
            ladder, kept, (((0, 2), (1, 2)), ((), ())), preferred_element_type=jnp.float32
        )
        return total

    return lax.map(one_virtual, jnp.moveaxis(left_piece, 1, 0))


def body(left_integrals, right_integrals, metric_factor, amplitudes, tile_sizes, pair_mask):
    aux_local = metric_factor.shape[0]
    aux_total = metric_factor.shape[1]
    a_local = left_integrals.shape[0]
    b_local = right_integrals.shape[0]
    c_width = amplitudes.shape[1]
    d_width = amplitudes.shape[2]
    pair_count = amplitudes.shape[0]
    c_offset = lax.axis_index("ab") * c_width
    d_offset = lax.axis_index("cd") * d_width
    left_count = a_local * c_width
    stacked = jnp.concatenate(
        [left_integrals.reshape(-1, aux_local), right_integrals.reshape(-1, aux_local)], axis=0
    )
    share = aux_total // lax.axis_size("aux")
    fitted = lax.psum_scatter(
        lax.dot_general(
            metric_factor, stacked, (((0,), (1,)), ((), ())), preferred_element_type=jnp.float32
        ),
        "aux",
        scatter_dimension=0,
        tiled=True,
    ).astype(jnp.bfloat16)
    left_fit = fitted[:, :left_count].reshape(share, a_local, c_width)
    right_fit = fitted[:, left_count:].reshape(share, b_local, d_width)
    right_all = lax.all_gather(right_fit, "ab", axis=1, tiled=True)
    keep_mask = region_keep(tile_sizes, pair_mask, c_offset, c_width, d_offset, d_width)
    kept = amplitudes * keep_mask.astype(jnp.bfloat16)[None]
    partial_sums = ladder_terms(lax.all_gather(left_fit, "cd", axis=1, tiled=True), right_all, kept)
    flat_terms = partial_sums.reshape(-1, pair_count)
    owned = lax.psum_scatter(flat_terms, ("cd", "ab"), scatter_dimension=0, tiled=True)
    totals = lax.psum(owned, "aux")
    return totals.reshape(a_local, b_local, pair_count)


def solution(mesh):
    return jax.shard_map(
        body,
        mesh=mesh,
        in_specs=(
            P("cd", "ab", "aux"),
            P("ab", "cd", "aux"),
            P("aux", None),
            P(None, "ab", "cd"),
            P(),
            P(),
        ),
        out_specs=P("cd", "ab", None),
        check_vma=False,
    )
```

profile of v0, /device:TPU:0, one launch (start us, length us, event | category | flops | bytes accessed | tf_op | source)
XLA Modules:
  0.0 353.8 jit_solution(16906253457313340899)
XLA Ops:
  6.5 0.0 copy-start
  6.5 0.0 reduce-scatter.2.cloned.1.call-start
  6.5 1.6 copy-done
  8.1 7.8 %convolution_bitcast_fusion.1 = f32[2048,1536]{0,1:T(8,128)} fusion(bf16[512,2048]{1,0:T(8,128)(2,1)S(1)} %copy-done, bf16[512,512]{1,0:T(8,128)(2,1)} %bitcast.43, bf16[1024,512]{1,0:T(8,128)(2,1)} %bitcast.42), kind=kOutput, calls=%fused_computation.7 | convolution fusion | flops 3224371200 | bytes 16252928 | tf_op jit(solution)/shard_map/dot_general | solution.py:58
  15.9 0.0 reduce-scatter.2.cloned.1.call-update
  15.9 0.0 all-gather.7.cloned.1.call-start
  16.0 100.0 %reduce-scatter.2.cloned.1.call-done = f32[512,1536]{0,1:T(8,128)} async-done(((f32[2048,1536]{0,1:T(8,128)}), f32[512,1536]{0,1:T(8,128)}) %reduce-scatter.2.cloned.1.call-update) | async-done | bytes 3145744 | tf_op jit(solution)/shard_map/reduce_scatter | solution.py:57
  116.0 2.1 convert_element_type.20
  118.1 0.0 copy-start.2
  118.1 0.0 copy-start.4
  118.1 0.0 copy-start.3
  118.1 0.9 slice.9
  118.9 0.0 all-gather.7.cloned.1.call-update
  119.0 0.0 all-gather.5.cloned.1.call-start
  119.0 1.0 slice.8
  120.0 0.0 all-gather.5.cloned.1.call-update
  120.1 0.0 copy-done.2
  120.1 0.1 copy.24
  120.2 0.1 reduce
  120.3 0.0 copy-done.4
  120.4 0.6 dynamic-slice
  120.9 0.1 convert_reduce_fusion.1
  121.0 0.1 convert_reduce_fusion
  121.1 0.0 copy-done.3
  121.1 0.5 fusion.7
  121.6 1.1 convolution_convert_fusion.1
  122.7 29.4 %copy_multiply_fusion = bf16[32,1024,512]{2,0,1:T(8,128)(2,1)} fusion(bf16[32,1024,512]{2,1,0:T(8,128)(2,1)} %param.11, bf16[1024,512]{1,0:T(8,128)(2,1)S(1)} %convolution_convert_fusion.1), kind=kLoop, calls=%fused_computation.6 | loop fusion | flops 16777216 | bytes 68157440 | tf_op jit(solution)/shard_map/mul | solution.py:69
  152.1 0.0 all-gather.7.cloned.1.call-done
  152.1 1.5 copy.26
  153.6 69.1 %all-gather.5.cloned.1.call-done = bf16[512,4096]{0,1:T(8,128)(2,1)} async-done(((bf16[512,1024]{0,1:T(8,128)(2,1)}), bf16[512,4096]{0,1:T(8,128)(2,1)}) %all-gather.5.cloned.1.call-update) | async-done | bytes 4194320 | tf_op jit(solution)/shard_map/all_gather | solution.py:70
  222.8 6.3 %copy.23 = bf16[512,4,1024]{2,0,1:T(8,128)(2,1)} copy(bf16[512,4,1024]{0,2,1:T(8,128)(2,1)} %bitcast.38) | data formatting | bytes 8388608 | tf_op jit(solution)/shard_map/all_gather | solution.py:70
  229.1 92.4 %while.10 = (s32[]{:T(128)}, f32[4,2,32]{2,1,0:T(2,128)S(1)}, bf16[4,512,1024]{2,1,0:T(8,128)(2,1)}, bf16[512,1024]{1,0:T(8,128)(2,1)S(1)}, bf16[32,1024,512]{2,0,1:T(8,128)(2,1)}, /*index=5*/s32[]{:T(128)}) while((s32[]{:T(128)}, f32[4,2,32]{2,1,0:T(2,128)S(1)}, bf16[4,512,1024]{2,1,0:T(8,128)(2,1)}, bf16[512,1024]{1,0:T(8,128)(2,1)S(1)}, ...), condition=%wide.region_5.6_spmd, body=%wide.region_4.5_spmd.sunk | while | flops 1141899264 | bytes 44041300 | solution.py:39
  229.1 3.8 %convolution_convert_fusion.3 = bf16[1024,1024]{0,1:T(8,128)(2,1)} fusion(bf16[512,1024]{1,0:T(8,128)(2,1)S(1)} %get-tuple-element.109, bf16[4,512,1024]{2,1,0:T(8,128)(2,1)} %get-tuple-element.108, s32[]{:T(128)S(6)} %copy.33), kind=kOutput, calls=%fused_computation.clone.1 | convolution fusion | flops 1074790400 | bytes 4194308 | tf_op jit(solution)/shard_map/while/body/eval_jaxpr/dot_general | solution.py:30
  232.9 4.8 %copy.29 = bf16[1024,2,512]{2,1,0:T(2,128)(2,1)S(1)} copy(bf16[1024,2,512]{0,2,1:T(8,128)(2,1)} %bitcast.37) | data formatting | bytes 4194304 | tf_op jit(solution)/shard_map/while/body/eval_jaxpr/reshape | solution.py:33
  237.8 14.4 %fusion.26 = f32[4,2,32]{2,1,0:T(2,128)S(1)} fusion(f32[4,2,32]{2,1,0:T(2,128)S(1)} %get-tuple-element.101, s32[]{:T(128)S(6)} %copy.33, bf16[1024,2,512]{2,1,0:T(2,128)(2,1)S(1)} %copy.29, bf16[32,1024,512]{2,0,1:T(8,128)(2,1)} %get-tuple-element.110), kind=kOutput, calls=%fused_computation.2.clone.1 | convolution fusion | flops 67108864 | bytes 35652612 | tf_op jit(solution)/shard_map/while/body/eval_jaxpr/dot_general | solution.py:34
  252.2 3.9 %convolution_convert_fusion.3 = bf16[1024,1024]{0,1:T(8,128)(2,1)} fusion(bf16[512,1024]{1,0:T(8,128)(2,1)S(1)} %get-tuple-element.109, bf16[4,512,1024]{2,1,0:T(8,128)(2,1)} %get-tuple-element.108, s32[]{:T(128)S(6)} %copy.33), kind=kOutput, calls=%fused_computation.clone.1 | convolution fusion | flops 1074790400 | bytes 4194308 | tf_op jit(solution)/shard_map/while/body/eval_jaxpr/dot_general | solution.py:30
  256.1 4.8 %copy.29 = bf16[1024,2,512]{2,1,0:T(2,128)(2,1)S(1)} copy(bf16[1024,2,512]{0,2,1:T(8,128)(2,1)} %bitcast.37) | data formatting | bytes 4194304 | tf_op jit(solution)/shard_map/while/body/eval_jaxpr/reshape | solution.py:33
  260.9 14.4 %fusion.26 = f32[4,2,32]{2,1,0:T(2,128)S(1)} fusion(f32[4,2,32]{2,1,0:T(2,128)S(1)} %get-tuple-element.101, s32[]{:T(128)S(6)} %copy.33, bf16[1024,2,512]{2,1,0:T(2,128)(2,1)S(1)} %copy.29, bf16[32,1024,512]{2,0,1:T(8,128)(2,1)} %get-tuple-element.110), kind=kOutput, calls=%fused_computation.2.clone.1 | convolution fusion | flops 67108864 | bytes 35652612 | tf_op jit(solution)/shard_map/while/body/eval_jaxpr/dot_general | solution.py:34
  275.3 3.9 %convolution_convert_fusion.3 = bf16[1024,1024]{0,1:T(8,128)(2,1)} fusion(bf16[512,1024]{1,0:T(8,128)(2,1)S(1)} %get-tuple-element.109, bf16[4,512,1024]{2,1,0:T(8,128)(2,1)} %get-tuple-element.108, s32[]{:T(128)S(6)} %copy.33), kind=kOutput, calls=%fused_computation.clone.1 | convolution fusion | flops 1074790400 | bytes 4194308 | tf_op jit(solution)/shard_map/while/body/eval_jaxpr/dot_general | solution.py:30
  279.2 4.8 %copy.29 = bf16[1024,2,512]{2,1,0:T(2,128)(2,1)S(1)} copy(bf16[1024,2,512]{0,2,1:T(8,128)(2,1)} %bitcast.37) | data formatting | bytes 4194304 | tf_op jit(solution)/shard_map/while/body/eval_jaxpr/reshape | solution.py:33
  284.0 14.4 %fusion.26 = f32[4,2,32]{2,1,0:T(2,128)S(1)} fusion(f32[4,2,32]{2,1,0:T(2,128)S(1)} %get-tuple-element.101, s32[]{:T(128)S(6)} %copy.33, bf16[1024,2,512]{2,1,0:T(2,128)(2,1)S(1)} %copy.29, bf16[32,1024,512]{2,0,1:T(8,128)(2,1)} %get-tuple-element.110), kind=kOutput, calls=%fused_computation.2.clone.1 | convolution fusion | flops 67108864 | bytes 35652612 | tf_op jit(solution)/shard_map/while/body/eval_jaxpr/dot_general | solution.py:34
  298.4 3.9 %convolution_convert_fusion.3 = bf16[1024,1024]{0,1:T(8,128)(2,1)} fusion(bf16[512,1024]{1,0:T(8,128)(2,1)S(1)} %get-tuple-element.109, bf16[4,512,1024]{2,1,0:T(8,128)(2,1)} %get-tuple-element.108, s32[]{:T(128)S(6)} %copy.33), kind=kOutput, calls=%fused_computation.clone.1 | convolution fusion | flops 1074790400 | bytes 4194308 | tf_op jit(solution)/shard_map/while/body/eval_jaxpr/dot_general | solution.py:30
  302.3 4.8 %copy.29 = bf16[1024,2,512]{2,1,0:T(2,128)(2,1)S(1)} copy(bf16[1024,2,512]{0,2,1:T(8,128)(2,1)} %bitcast.37) | data formatting | bytes 4194304 | tf_op jit(solution)/shard_map/while/body/eval_jaxpr/reshape | solution.py:33
  307.1 14.4 %fusion.26 = f32[4,2,32]{2,1,0:T(2,128)S(1)} fusion(f32[4,2,32]{2,1,0:T(2,128)S(1)} %get-tuple-element.101, s32[]{:T(128)S(6)} %copy.33, bf16[1024,2,512]{2,1,0:T(2,128)(2,1)S(1)} %copy.29, bf16[32,1024,512]{2,0,1:T(8,128)(2,1)} %get-tuple-element.110), kind=kOutput, calls=%fused_computation.2.clone.1 | convolution fusion | flops 67108864 | bytes 35652612 | tf_op jit(solution)/shard_map/while/body/eval_jaxpr/dot_general | solution.py:34
  321.6 0.0 copy-start.1
  321.6 19.0 %all-reduce = f32[8,32]{1,0:T(8,128)S(1)} all-reduce(f32[8,32]{1,0:T(8,128)S(1)} %bitcast.40), channel_id=5, replica_groups=mesh['aux'=4,'cd'=4,'ab'=2] {'cd','ab'}, use_global_device_ids=true, to_apply=%region_6.7.clone | all-reduce | flops 256 | bytes 2048
  340.5 0.6 dynamic-slice_bitcast_fusion
  341.1 6.2 %psum.7 = f32[1,1,32]{2,1,0:T(1,128)} all-reduce(f32[1,1,32]{2,1,0:T(1,128)S(1)} %dynamic-slice_bitcast_fusion), channel_id=1, replica_groups=mesh['aux'=4,'cd'=4,'ab'=2] {'aux'}, use_global_device_ids=true, to_apply=%region_7.8 | all-reduce | flops 32 | bytes 256 | tf_op jit(solution)/shard_map/psum | solution.py:73
  347.2 0.0 copy-done.1
  (4 shorter events, 0.0 us)
Async XLA Ops:
  6.5 1.6 copy-start
  6.5 109.4 %reduce-scatter.2.cloned.1.call-start = ((), (), s32[]{:S(2)}) async-start(), calls=%async_computation.1 | async-start | bytes 15728640 | tf_op jit(solution)/shard_map/reduce_scatter | solution.py:57
  15.9 136.2 %all-gather.7.cloned.1.call-start = ((), (), s32[]{:S(2)}) async-start(), calls=%async_computation.3 | async-start | bytes 1572864 | tf_op jit(solution)/shard_map/all_gather | solution.py:67
  118.1 2.0 copy-start.2
  118.1 2.3 copy-start.4
  118.1 3.0 copy-start.3
  119.0 103.8 %all-gather.5.cloned.1.call-start = ((), (), s32[]{:S(2)}) async-start(), calls=%async_computation.2 | async-start | bytes 5242880 | tf_op jit(solution)/shard_map/all_gather | solution.py:70
  321.6 25.7 %copy-start.1 = (bf16[512,2048]{1,0:T(8,128)(2,1)S(1)}, bf16[512,2048]{1,0:T(8,128)(2,1)}, u32[]{:S(2)}) copy-start(bf16[512,2048]{1,0:T(8,128)(2,1)} %param.10) | copy-start | bytes 6291460
Sparse Core Ops, SparseCore 0:
  16.1 99.8 reduce-scatter.1
  119.1 21.2 all-gather.6
  142.0 80.7 all-gather.4
where the time goes:
time: 355 us; the launch traced here: 354 us
  waiting for transfers between devices  169 us (48%)
  matrix products  82.5 us (23%)
  local copies, waits for them, and re-layouts  31.8 us (9%)
  other arithmetic  31.8 us (9%)
  blocking collectives  25.1 us (7%)
  between operations  13.2 us (4%)
    reduce_scatter x1, waiting for transfers between devices, body(): lax.psum_scatter(lax.dot_general(metric_factor, stacked, (((0,), (1,)), (...  100 us
    all_gather x1, waiting for transfers between devices, body(): lax.all_gather(left_fit, 'cd', axis=1, tiled=True)  69.1 us
    dot_general x4, matrix products, one_virtual(): lax.dot_general(ladder, kept, (((0, 2), (1, 2)), ((), ())), preferred_ele...  57.7 us
    mul x1, other arithmetic, body(): kept = amplitudes * keep_mask.astype(jnp.bfloat16)[None]  29.4 us
    reshape x4, local copies, waits for them, and re-layouts, one_virtual(): ladder = ladder.astype(jnp.bfloat16).reshape(-1, b_count, d_width)  19.3 us
    unnamed x1, blocking collectives  19 us
    dot_general x4, matrix products, one_virtual(): lax.dot_general(left_slab, right_flat, (((0,), (0,)), ((), ())), preferre...  15.4 us
    dot_general x1, matrix products, body(): lax.dot_general(metric_factor, stacked, (((0,), (1,)), ((), ())), preferr...  7.79 us
  transfers between devices with their start and end apart: 3, of which 2 were waited for; matrix products, arithmetic and copies ran while one was open for 10% of the time, Pallas kernels for 0%

commit v1 on v0

--- a/solution.py
+++ b/solution.py
@@ -2,6 +2,24 @@
 import jax.numpy as jnp
 from jax import lax
 from jax.sharding import PartitionSpec as P
+
+
+def gather_around(array, axis, dim):
+    ways, here, turn = (lax.axis_size(axis), lax.axis_index(axis), array.shape[dim])
+    dims = [n * ways if d == dim else n for d, n in enumerate(array.shape)]
+    full = lax.dynamic_update_slice_in_dim(
+        jnp.zeros(dims, array.dtype), array, here * turn, axis=dim
+    )
+    going_up = going_down = array
+    for far in range(1, ways // 2 + 1):
+        going_up = lax.ppermute(going_up, axis, [(d, (d + 1) % ways) for d in range(ways)])
+        full = lax.dynamic_update_slice_in_dim(full, going_up, (here - far) % ways * turn, axis=dim)
+        if 2 * far < ways:
+            going_down = lax.ppermute(going_down, axis, [(d, (d - 1) % ways) for d in range(ways)])
+            full = lax.dynamic_update_slice_in_dim(
+                full, going_down, (here + far) % ways * turn, axis=dim
+            )
+    return full
 
 
 def region_keep(tile_sizes, pair_mask, c_offset, c_count, d_offset, d_count):
@@ -67,7 +85,7 @@
     right_all = lax.all_gather(right_fit, "ab", axis=1, tiled=True)
     keep_mask = region_keep(tile_sizes, pair_mask, c_offset, c_width, d_offset, d_width)
     kept = amplitudes * keep_mask.astype(jnp.bfloat16)[None]
-    partial_sums = ladder_terms(lax.all_gather(left_fit, "cd", axis=1, tiled=True), right_all, kept)
+    partial_sums = ladder_terms(gather_around(left_fit, "cd", 1), right_all, kept)
     flat_terms = partial_sums.reshape(-1, pair_count)
     owned = lax.psum_scatter(flat_terms, ("cd", "ab"), scatter_dimension=0, tiled=True)
     totals = lax.psum(owned, "aux")

time: 355 us -> 321 us (0.904)
  waiting for transfers between devices: 169 us -> 123 us
  local copies, waits for them, and re-layouts: 31.8 us -> 38.4 us
  starting transfers between devices: 0.09 us -> 3.92 us
    all_gather x1 -> x0, waiting for transfers between devices: 69.1 us -> none  [body(): lax.all_gather(left_fit, 'cd', axis=1, tiled=True)]
    ppermute x0 -> x3, waiting for transfers between devices: none -> 23.2 us  [the longest x2 23.2 us: gather_around(): lax.ppermute(going_up, axis, [(d, (d + 1) % ways) for d in range(ways)])]
    all_gather x1 -> x0, local copies, waits for them, and re-layouts: 6.35 us -> none  [body(): lax.all_gather(left_fit, 'cd', axis=1, tiled=True)]
    ppermute x0 -> x3, local copies, waits for them, and re-layouts: none -> 4.45 us  [the longest x2 2.96 us: gather_around(): lax.ppermute(going_up, axis, [(d, (d + 1) % ways) for d in range(ways)])]
    dynamic_update_slice x0 -> x4, local copies, waits for them, and re-layouts: none -> 4.27 us  [the longest x2 2.14 us: gather_around(): lax.dynamic_update_slice_in_dim(full, going_up, (here - far) % ways * tur...]
    ppermute x0 -> x3, starting transfers between devices: none -> 3.88 us  [the longest x1 2.39 us: gather_around(): lax.ppermute(going_down, axis, [(d, (d - 1) % ways) for d in range(ways)])]
  transfers between devices with their start and end apart: 3 -> 5, of which waited for: 2 -> 3; matrix products, arithmetic and copies ran while one was open for 10% -> 14% of each run, Pallas kernels for 0% -> 0%
where the time goes in v1:
time: 321 us; the launch traced here: 320 us
  waiting for transfers between devices  123 us (38%)
  matrix products  82.5 us (26%)
  local copies, waits for them, and re-layouts  38.4 us (12%)
  other arithmetic  31.8 us (10%)
  blocking collectives  26.6 us (8%)
  between operations  13.5 us (4%)
  starting transfers between devices  3.92 us (1%)
    reduce_scatter x1, waiting for transfers between devices, body(): lax.psum_scatter(lax.dot_general(metric_factor, stacked, (((0,), (1,)), (...  100 us
    dot_general x4, matrix products, one_virtual(): lax.dot_general(ladder, kept, (((0, 2), (1, 2)), ((), ())), preferred_ele...  57.7 us
    mul x1, other arithmetic, body(): kept = amplitudes * keep_mask.astype(jnp.bfloat16)[None]  29.4 us
    ppermute x2, waiting for transfers between devices, gather_around(): lax.ppermute(going_up, axis, [(d, (d + 1) % ways) for d in range(ways)])  23.2 us
    unnamed x1, blocking collectives  20.2 us
    reshape x4, local copies, waits for them, and re-layouts, one_virtual(): ladder = ladder.astype(jnp.bfloat16).reshape(-1, b_count, d_width)  19.3 us
    dot_general x4, matrix products, one_virtual(): lax.dot_general(left_slab, right_flat, (((0,), (0,)), ((), ())), preferre...  15.3 us
    dot_general x1, matrix products, body(): lax.dot_general(metric_factor, stacked, (((0,), (1,)), ((), ())), preferr...  7.79 us
  transfers between devices with their start and end apart: 5, of which 3 were waited for; matrix products, arithmetic and copies ran while one was open for 14% of the time, Pallas kernels for 0%

profile of v1, /device:TPU:0, one launch (start us, length us, event | category | flops | bytes accessed | tf_op | source)
XLA Modules:
  0.0 320.0 jit_solution(627002419919514737)
XLA Ops:
  6.5 0.0 copy-start
  6.5 0.0 reduce-scatter.2.cloned.1.call-start
  6.5 1.6 copy-done
  8.1 7.8 %convolution_bitcast_fusion.1 = f32[2048,1536]{0,1:T(8,128)} fusion(bf16[512,2048]{1,0:T(8,128)(2,1)S(1)} %copy-done, bf16[512,512]{1,0:T(8,128)(2,1)} %bitcast.42, bf16[1024,512]{1,0:T(8,128)(2,1)} %bitcast.41), kind=kOutput, calls=%fused_computation.7 | convolution fusion | flops 3224371200 | bytes 16252928 | tf_op jit(solution)/shard_map/dot_general | solution.py:76
  15.9 0.0 reduce-scatter.2.cloned.1.call-update
  15.9 0.0 copy-start.2
  15.9 0.0 copy-start.3
  16.0 0.0 all-gather.3.cloned.1.call-start
  16.0 100.0 %reduce-scatter.2.cloned.1.call-done = f32[512,1536]{0,1:T(8,128)} async-done(((f32[2048,1536]{0,1:T(8,128)}), f32[512,1536]{0,1:T(8,128)}) %reduce-scatter.2.cloned.1.call-update) | async-done | bytes 3145744 | tf_op jit(solution)/shard_map/reduce_scatter | solution.py:75
  116.0 2.1 convert_element_type.20
  118.1 1.1 slice_bitcast_fusion
  119.1 1.5 collective-permute-start
  120.6 0.0 copy-done.2
  120.6 0.1 copy.36
  120.7 0.1 reduce
  120.9 0.1 convert_reduce_fusion.1
  121.0 0.1 convert_reduce_fusion
  121.0 0.0 copy-done.3
  121.1 0.5 fusion.7
  121.5 1.1 convolution_convert_fusion.1
  122.6 2.4 collective-permute-start.1
  125.0 0.8 slice.9
  125.9 0.0 all-gather.3.cloned.1.call-update
  125.9 0.0 copy-start.4
  125.9 21.4 %collective-permute-done = bf16[512,1,1024]{0,2,1:T(8,128)(2,1)} collective-permute-done((bf16[512,1,1024]{0,2,1:T(8,128)(2,1)}, bf16[512,1,1024]{0,2,1:T(8,128)(2,1)}, u32[]{:S(2)}, u32[]{:S(2)}) %collective-permute-start) | collective-permute-done | bytes 1048608 | tf_op jit(solution)/shard_map/ppermute | solution.py:15
  147.3 0.0 collective-permute-start.2
  147.3 29.4 %copy_multiply_fusion = bf16[32,1024,512]{2,0,1:T(8,128)(2,1)} fusion(bf16[32,1024,512]{2,1,0:T(8,128)(2,1)} %param.11, bf16[1024,512]{1,0:T(8,128)(2,1)S(1)} %convolution_convert_fusion.1), kind=kLoop, calls=%fused_computation.6 | loop fusion | flops 16777216 | bytes 68157440 | tf_op jit(solution)/shard_map/mul | solution.py:87
  176.7 0.0 copy-done.4
  176.7 0.6 dynamic-slice
  177.3 1.5 copy.32
  178.8 2.6 broadcast_in_dim.8
  181.4 1.1 constant_dynamic-update-slice_fusion.3
  182.5 1.5 copy.33
  183.9 0.0 collective-permute-done.1
  184.0 1.5 copy.34
  185.5 0.0 all-gather.3.cloned.1.call-done
  185.5 1.5 copy.38
  187.0 1.1 constant_dynamic-update-slice_fusion.2
  188.1 1.1 constant_dynamic-update-slice_fusion.1
  189.1 1.8 collective-permute-done.2
  191.0 1.5 copy.35
  192.5 1.1 constant_dynamic-update-slice_fusion
  193.5 92.4 %while.10 = (s32[]{:T(128)}, f32[4,2,32]{2,1,0:T(2,128)S(1)}, bf16[4,512,1024]{2,1,0:T(8,128)(2,1)}, bf16[512,1024]{1,0:T(8,128)(2,1)S(1)}, bf16[32,1024,512]{2,0,1:T(8,128)(2,1)}, /*index=5*/s32[]{:T(128)}) while((s32[]{:T(128)}, f32[4,2,32]{2,1,0:T(2,128)S(1)}, bf16[4,512,1024]{2,1,0:T(8,128)(2,1)}, bf16[512,1024]{1,0:T(8,128)(2,1)S(1)}, ...), condition=%wide.region_5.6_spmd, body=%wide.region_4.5_spmd.sunk | while | flops 1141899264 | bytes 44041800 | solution.py:57
  193.5 3.8 %convolution_convert_fusion.3 = bf16[1024,1024]{0,1:T(8,128)(2,1)} fusion(bf16[512,1024]{1,0:T(8,128)(2,1)S(1)} %get-tuple-element.109, bf16[4,512,1024]{2,1,0:T(8,128)(2,1)} %get-tuple-element.108, s32[]{:T(128)} %get-tuple-element.100), kind=kOutput, calls=%fused_computation.clone.1 | convolution fusion | flops 1074790400 | bytes 4194816 | tf_op jit(solution)/shard_map/while/body/eval_jaxpr/dot_general | solution.py:48
  197.3 4.8 %copy.41 = bf16[1024,2,512]{2,1,0:T(2,128)(2,1)S(1)} copy(bf16[1024,2,512]{0,2,1:T(8,128)(2,1)} %bitcast.38) | data formatting | bytes 4194304 | tf_op jit(solution)/shard_map/while/body/eval_jaxpr/reshape | solution.py:51
  202.2 14.4 %fusion.26 = f32[4,2,32]{2,1,0:T(2,128)S(1)} fusion(f32[4,2,32]{2,1,0:T(2,128)S(1)} %get-tuple-element.101, s32[]{:T(128)} %get-tuple-element.100, bf16[1024,2,512]{2,1,0:T(2,128)(2,1)S(1)} %copy.41, bf16[32,1024,512]{2,0,1:T(8,128)(2,1)} %get-tuple-element.110), kind=kOutput, calls=%fused_computation.2.clone.1 | convolution fusion | flops 67108864 | bytes 35652612 | tf_op jit(solution)/shard_map/while/body/eval_jaxpr/dot_general | solution.py:52
  216.6 3.8 %convolution_convert_fusion.3 = bf16[1024,1024]{0,1:T(8,128)(2,1)} fusion(bf16[512,1024]{1,0:T(8,128)(2,1)S(1)} %get-tuple-element.109, bf16[4,512,1024]{2,1,0:T(8,128)(2,1)} %get-tuple-element.108, s32[]{:T(128)} %get-tuple-element.100), kind=kOutput, calls=%fused_computation.clone.1 | convolution fusion | flops 1074790400 | bytes 4194816 | tf_op jit(solution)/shard_map/while/body/eval_jaxpr/dot_general | solution.py:48
  220.4 4.8 %copy.41 = bf16[1024,2,512]{2,1,0:T(2,128)(2,1)S(1)} copy(bf16[1024,2,512]{0,2,1:T(8,128)(2,1)} %bitcast.38) | data formatting | bytes 4194304 | tf_op jit(solution)/shard_map/while/body/eval_jaxpr/reshape | solution.py:51
  225.3 14.4 %fusion.26 = f32[4,2,32]{2,1,0:T(2,128)S(1)} fusion(f32[4,2,32]{2,1,0:T(2,128)S(1)} %get-tuple-element.101, s32[]{:T(128)} %get-tuple-element.100, bf16[1024,2,512]{2,1,0:T(2,128)(2,1)S(1)} %copy.41, bf16[32,1024,512]{2,0,1:T(8,128)(2,1)} %get-tuple-element.110), kind=kOutput, calls=%fused_computation.2.clone.1 | convolution fusion | flops 67108864 | bytes 35652612 | tf_op jit(solution)/shard_map/while/body/eval_jaxpr/dot_general | solution.py:52
  239.7 3.8 %convolution_convert_fusion.3 = bf16[1024,1024]{0,1:T(8,128)(2,1)} fusion(bf16[512,1024]{1,0:T(8,128)(2,1)S(1)} %get-tuple-element.109, bf16[4,512,1024]{2,1,0:T(8,128)(2,1)} %get-tuple-element.108, s32[]{:T(128)} %get-tuple-element.100), kind=kOutput, calls=%fused_computation.clone.1 | convolution fusion | flops 1074790400 | bytes 4194816 | tf_op jit(solution)/shard_map/while/body/eval_jaxpr/dot_general | solution.py:48
  243.5 4.8 %copy.41 = bf16[1024,2,512]{2,1,0:T(2,128)(2,1)S(1)} copy(bf16[1024,2,512]{0,2,1:T(8,128)(2,1)} %bitcast.38) | data formatting | bytes 4194304 | tf_op jit(solution)/shard_map/while/body/eval_jaxpr/reshape | solution.py:51
  248.3 14.4 %fusion.26 = f32[4,2,32]{2,1,0:T(2,128)S(1)} fusion(f32[4,2,32]{2,1,0:T(2,128)S(1)} %get-tuple-element.101, s32[]{:T(128)} %get-tuple-element.100, bf16[1024,2,512]{2,1,0:T(2,128)(2,1)S(1)} %copy.41, bf16[32,1024,512]{2,0,1:T(8,128)(2,1)} %get-tuple-element.110), kind=kOutput, calls=%fused_computation.2.clone.1 | convolution fusion | flops 67108864 | bytes 35652612 | tf_op jit(solution)/shard_map/while/body/eval_jaxpr/dot_general | solution.py:52
  262.8 3.8 %convolution_convert_fusion.3 = bf16[1024,1024]{0,1:T(8,128)(2,1)} fusion(bf16[512,1024]{1,0:T(8,128)(2,1)S(1)} %get-tuple-element.109, bf16[4,512,1024]{2,1,0:T(8,128)(2,1)} %get-tuple-element.108, s32[]{:T(128)} %get-tuple-element.100), kind=kOutput, calls=%fused_computation.clone.1 | convolution fusion | flops 1074790400 | bytes 4194816 | tf_op jit(solution)/shard_map/while/body/eval_jaxpr/dot_general | solution.py:48
  266.6 4.8 %copy.41 = bf16[1024,2,512]{2,1,0:T(2,128)(2,1)S(1)} copy(bf16[1024,2,512]{0,2,1:T(8,128)(2,1)} %bitcast.38) | data formatting | bytes 4194304 | tf_op jit(solution)/shard_map/while/body/eval_jaxpr/reshape | solution.py:51
  271.4 14.4 %fusion.26 = f32[4,2,32]{2,1,0:T(2,128)S(1)} fusion(f32[4,2,32]{2,1,0:T(2,128)S(1)} %get-tuple-element.101, s32[]{:T(128)} %get-tuple-element.100, bf16[1024,2,512]{2,1,0:T(2,128)(2,1)S(1)} %copy.41, bf16[32,1024,512]{2,0,1:T(8,128)(2,1)} %get-tuple-element.110), kind=kOutput, calls=%fused_computation.2.clone.1 | convolution fusion | flops 67108864 | bytes 35652612 | tf_op jit(solution)/shard_map/while/body/eval_jaxpr/dot_general | solution.py:52
  285.9 0.0 copy-start.1
  285.9 20.2 %all-reduce = f32[8,32]{1,0:T(8,128)S(1)} all-reduce(f32[8,32]{1,0:T(8,128)S(1)} %bitcast.39), channel_id=4, replica_groups=mesh['aux'=4,'cd'=4,'ab'=2] {'cd','ab'}, use_global_device_ids=true, to_apply=%region_6.7.clone | all-reduce | flops 256 | bytes 2048
  306.1 0.6 dynamic-slice_bitcast_fusion
  306.7 6.4 %psum.7 = f32[1,1,32]{2,1,0:T(1,128)} all-reduce(f32[1,1,32]{2,1,0:T(1,128)S(1)} %dynamic-slice_bitcast_fusion), channel_id=1, replica_groups=mesh['aux'=4,'cd'=4,'ab'=2] {'aux'}, use_global_device_ids=true, to_apply=%region_7.8 | all-reduce | flops 32 | bytes 256 | tf_op jit(solution)/shard_map/psum | solution.py:91
  313.1 0.0 copy-done.1
  (4 shorter events, 0.0 us)
Async XLA Ops:
  6.5 1.6 copy-start
  6.5 109.4 %reduce-scatter.2.cloned.1.call-start = ((), (), s32[]{:S(2)}) async-start(), calls=%async_computation.1 | async-start | bytes 15728640 | tf_op jit(solution)/shard_map/reduce_scatter | solution.py:75
  15.9 104.7 %copy-start.2 = (s32[16]{0:T(128)S(1)}, s32[16]{0:T(128)}, u32[]{:S(2)}) copy-start(s32[16]{0:T(128)} %param.12) | copy-start | bytes 196
  15.9 105.1 %copy-start.3 = (s32[16,16]{1,0:T(8,128)S(1)}, s32[16,16]{1,0:T(8,128)}, u32[]{:S(2)}) copy-start(s32[16,16]{1,0:T(8,128)} %param.13) | copy-start | bytes 3076
  16.0 169.5 %all-gather.3.cloned.1.call-start = ((), (), s32[]{:S(2)}) async-start(), calls=%async_computation.2 | async-start | bytes 1572864 | tf_op jit(solution)/shard_map/all_gather | solution.py:85
  119.1 28.2 %collective-permute-start = (bf16[512,1,1024]{0,2,1:T(8,128)(2,1)}, bf16[512,1,1024]{0,2,1:T(8,128)(2,1)}, u32[]{:S(2)}, u32[]{:S(2)}) collective-permute-start(bf16[512,1,1024]{0,2,1:T(8,128)(2,1)} %slice_bitcast_fusion), channel_id=1, source_target_pairs={{0,2},{2,4},{4,6},{6,0},{1,3},{3,5},{5,7},{7,1},{8,10},{10,12},{12... | collective-permute-start | bytes 3145736 | tf_op jit(solution)/shard_map/ppermute | solution.py:15
  122.6 61.3 %collective-permute-start.1 = (bf16[512,1,1024]{0,2,1:T(8,128)(2,1)}, bf16[512,1,1024]{0,2,1:T(8,128)(2,1)}, u32[]{:S(2)}, u32[]{:S(2)}) collective-permute-start(bf16[512,1,1024]{0,2,1:T(8,128)(2,1)} %slice_bitcast_fusion), channel_id=1, source_target_pairs={{0,6},{2,0},{4,2},{6,4},{1,7},{3,1},{5,3},{7,5},{8,14},{10,8},{12,... | collective-permute-start | bytes 3145736 | tf_op jit(solution)/shard_map/ppermute | solution.py:18
  125.9 50.8 %copy-start.4 = (u32[32]{0:T(128)S(1)}, u32[32]{0:T(128)}, u32[]{:S(2)}) copy-start(u32[32]{0:T(128)} %constant.61) | copy-start | bytes 388
  147.3 43.7 %collective-permute-start.2 = (bf16[512,1,1024]{0,2,1:T(8,128)(2,1)}, bf16[512,1,1024]{0,2,1:T(8,128)(2,1)}, u32[]{:S(2)}, u32[]{:S(2)}) collective-permute-start(bf16[512,1,1024]{0,2,1:T(8,128)(2,1)} %collective-permute-done), channel_id=1, source_target_pairs={{0,2},{2,4},{4,6},{6,0},{1,3},{3,5},{5,7},{7,1},{8,10},{10,12},{12... | collective-permute-start | bytes 3145736 | tf_op jit(solution)/shard_map/ppermute | solution.py:15
  285.9 27.2 %copy-start.1 = (bf16[512,2048]{1,0:T(8,128)(2,1)S(1)}, bf16[512,2048]{1,0:T(8,128)(2,1)}, u32[]{:S(2)}) copy-start(bf16[512,2048]{1,0:T(8,128)(2,1)} %param.10) | copy-start | bytes 6291460
Sparse Core Ops, SparseCore 0:
  16.1 99.8 reduce-scatter.1
  126.0 19.4 all-gather.2
